TPU v7x, 32 devices: a whole 2x2x4 slice. The times are simulated.
32 devices in a mesh: grp: 2 (over y), tok: 16 (over z, x, core).
Axes of the slice: x: 2, y: 2, z: 4, core: 2. Of those that a mesh axis runs over, the one named last changes fastest.
Arguments:
- hidden: bfloat16 [4, 1024, 1536], P('grp', 'tok'), parts along dimension 0
- base_ids: int32 [4, 1024], P('grp', 'tok'), parts along dimension 0, may hold values from 0 to 4, as said below
- attn_gain: bfloat16 [1536], replicated, may hold values from 0.099609375 to 1.8984375
- q_weight: bfloat16 [1536, 768], replicated
- kv_weight: bfloat16 [1536, 384], replicated
- out_weight: bfloat16 [768, 1536], replicated, may hold values from -0.21875 to 0.21875
- head_gain: bfloat16 [1536], replicated, may hold values from 0.099609375 to 1.8984375
- head_weight: bfloat16 [1536, 1536], replicated, may hold values from -0.15625 to 0.15625
- head_bias: float32 [1536], replicated, may hold values from -1 to 1
- track_perm: int32 [1536], replicated, may hold values from 0 to 1535, each once
Outputs:
- combined: float32 [2048, 1536], P(('grp', 'tok')), parts along dimension 0
There are 2 independent parts, one for each index of `grp`. A program takes and returns all parts, laid end to end along the dimension named above; an argument that names none is the same for every part. Nothing has to cross between parts.
Inputs may be any that keep to these rules, and one draw needn't show every extreme that they name: `base_ids`: every eighth token of each strand, from token 0, has a base 0 to 3.
All inputs are finite; a program needn't handle non-finite values.
Results may differ from a plain program's by a relative error of at most 0.0058.
Values may be sent and summed in bfloat16 or wider, within the bound.
No kernel may reach another device: no remote copies, remote signals or barrier semaphores. Data moves between devices by JAX's collectives and lax.ppermute only.
A program may use at most 128 MiB of HBM per device.

v0:
```python
import math

import jax
import jax.numpy as jnp
from jax import lax
from jax.sharding import PartitionSpec as P


def swapped(value, axis, distance):
    mask = 2**distance
    pairs = [(source, source ^ mask) for source in range(lax.axis_size(axis))]
    return lax.ppermute(value, axis, pairs)


def normalize(rows, gain):
    widened = rows.astype(jnp.float32)
    return (
        widened
        * lax.rsqrt(jnp.mean(widened * widened, -1, keepdims=True) + 1e-06)
        * gain.astype(jnp.float32)
    )


def attend(running, queries, key_value, usable_flag):
    maxima, totals, accumulated = running
    width_head = queries.shape[2]
    key_rows = key_value[:, :, :width_head]
    value_rows = key_value[:, :, width_head:]
    scores = jnp.einsum("srd,skd->srk", queries, key_rows, preferred_element_type=jnp.float32) * (
        1.0 / math.sqrt(width_head)
    )
    usable = usable_flag[:, None, :] > 0
    scores = jnp.where(usable, scores, jnp.float32(-1e30))
    new_maxima = jnp.maximum(maxima, jnp.max(scores, -1))
    weight_exp = jnp.where(usable, jnp.exp(scores - new_maxima[:, :, None]), jnp.float32(0.0))
    totals = jnp.sum(weight_exp, -1)
    summed = jnp.einsum(
        "srk,skd->srd",
        weight_exp.astype(jnp.bfloat16),
        value_rows,
        preferred_element_type=jnp.float32,
    )
    accumulated = summed
    return (new_maxima, totals, accumulated)


def per_device(
    hidden,
    base_ids,
    attn_gain,
    q_weight,
    kv_weight,
    out_weight,
    head_gain,
    head_weight,
    head_bias,
    track_perm,
):
    tok_rows = hidden.shape[1]
    width_head = kv_weight.shape[1] // 2
    head_count = q_weight.shape[1] // width_head
    bit_count = lax.axis_size("tok").bit_length() - 1
    normed = normalize(hidden, attn_gain).astype(jnp.bfloat16)
    key_value = jnp.einsum(
        "std,de->ste", normed, kv_weight, preferred_element_type=jnp.float32
    ).astype(jnp.bfloat16)
    usable_flag = (base_ids != 4).astype(jnp.bfloat16)
    partner = hidden[1]
    for bit_number in range(bit_count):
        partner = swapped(partner, "tok", bit_number)
    partner = partner[::-1]
    query_source = jnp.stack([normed[0], normalize(partner, attn_gain).astype(jnp.bfloat16)])
    residual_base = jnp.stack([hidden[0], partner])
    queries = jnp.einsum(
        "std,de->ste", query_source, q_weight, preferred_element_type=jnp.float32
    ).astype(jnp.bfloat16)
    queries = queries.reshape(2, tok_rows * head_count, width_head)
    row_count = queries.shape[1]
    start_state = (
        jnp.full((2, row_count), -1e30, jnp.float32),
        jnp.zeros((2, row_count), jnp.float32),
        jnp.zeros((2, row_count, width_head), jnp.float32),
    )
    softmax_state = attend(
        start_state,
        queries,
        lax.all_gather(key_value, "tok", axis=1, tiled=True),
        lax.all_gather(usable_flag, "tok", axis=1, tiled=True),
    )
    maxima, totals, accumulated = softmax_state
    attended = (
        (accumulated / totals[:, :, None])
        .astype(jnp.bfloat16)
        .reshape(2, tok_rows, head_count * width_head)
    )
    residual_sum = residual_base.astype(jnp.float32) + jnp.einsum(
        "ste,ed->std", attended, out_weight, preferred_element_type=jnp.float32
    )
    normed_out = normalize(residual_sum, head_gain).astype(jnp.bfloat16)
    forward_logits = (
        jnp.dot(normed_out[0], head_weight, preferred_element_type=jnp.float32) + head_bias
    )
    reverse_logits = (
        jnp.dot(normed_out[1], head_weight[:, track_perm], preferred_element_type=jnp.float32)
        + head_bias[track_perm]
    )
    forward_pred = jax.nn.softplus(forward_logits).astype(jnp.bfloat16)
    reverse_pred = jax.nn.softplus(reverse_logits).astype(jnp.bfloat16)
    return 0.5 * (forward_pred.astype(jnp.float32) + reverse_pred.astype(jnp.float32))


def solution(mesh):
    placed = (P("grp", "tok", None), P("grp", "tok"), P(), P(), P(), P(), P(), P(), P(), P())
    return jax.shard_map(
        per_device, mesh=mesh, in_specs=placed, out_specs=P(("grp", "tok"), None), check_vma=False
    )
```

profile of v0, /device:TPU:0, one launch (start us, length us, event | category | flops | bytes accessed | tf_op | source)
XLA Modules:
  0.0 101.3 jit_solution(12420879725566651075)
XLA Ops:
  6.5 0.0 copy-start
  6.5 0.0 copy-start.2
  6.5 0.0 copy-start.7
  6.5 0.0 all-gather.3.cloned.1.call-start
  6.6 0.8 convert_element_type.55
  7.4 1.2 %fusion.25 = f32[2,64]{1,0:T(2,128)S(1)} fusion(bf16[2,64,1536]{2,1,0:T(8,128)(2,1)} %param.10), kind=kLoop, calls=%fused_computation.31 | loop fusion | flops 589696 | bytes 393728 | tf_op jit(solution)/shard_map/reduce_sum | solution.py:19
  8.6 1.2 %fusion.27 = bf16[2,64,1536]{2,1,0:T(8,128)(2,1)S(1)} fusion(bf16[2,64,1536]{2,1,0:T(8,128)(2,1)} %param.10, f32[1536]{0:T(1024)S(1)} %convert_element_type.55, f32[2,64]{1,0:T(2,128)S(1)} %add_rsqrt_fusion.1), kind=kLoop, calls=%fused_computation.33 | loop fusion | flops 786432 | bytes 793088 | tf_op jit(solution)/shard_map/convert_element_type | solution.py:63
  9.8 0.0 copy-start.3
  9.8 2.4 %fusion.13 = bf16[2,64,384]{2,1,0:T(8,128)(2,1)} fusion(bf16[2,64,1536]{2,1,0:T(8,128)(2,1)S(1)} %fusion.27, bf16[1536,384]{1,0:T(8,128)(2,1)} %param.14), kind=kOutput, calls=%fused_computation.20 | convolution fusion | flops 151044096 | bytes 1671168 | tf_op jit(solution)/shard_map/std,de->ste/dot_general | solution.py:64
  12.2 0.0 all-gather.3.cloned.1.call-update
  12.2 0.0 copy-done.2
  12.3 0.6 collective-permute-start
  12.8 1.1 %collective-permute-done = bf16[64,1536]{1,0:T(8,128)(2,1)S(1)} collective-permute-done((bf16[64,1536]{1,0:T(8,128)(2,1)S(1)}, bf16[64,1536]{1,0:T(8,128)(2,1)S(1)}, u32[]{:S(2)}, u32[]{:S(2)}) %collective-permute-start) | collective-permute-done | bytes 196640 | tf_op jit(solution)/shard_map/ppermute | solution.py:12
  13.9 2.8 %collective-permute-start.1 = (bf16[64,1536]{1,0:T(8,128)(2,1)S(1)}, bf16[64,1536]{1,0:T(8,128)(2,1)S(1)}, u32[]{:S(2)}, u32[]{:S(2)}) collective-permute-start(bf16[64,1536]{1,0:T(8,128)(2,1)S(1)} %collective-permute-done), channel_id=1, source_target_pairs={{0,2},{1,3},{2,0},{3,1},{4,6},{5,7},{6,4},{7,5},{8,10},{9,11},{10,... | collective-permute-start | bytes 589832 | tf_op jit(solution)/shard_map/ppermute | solution.py:12
  16.7 0.0 copy-done.7
  16.7 20.7 %all-gather = bf16[16,64,2]{1,2,0:T(2,128)(2,1)S(1)} all-gather(bf16[1,64,2]{1,2,0:T(2,128)(2,1)S(1)} %fusion.37), channel_id=1, replica_groups=mesh['grp'=2,'tok'=16] {'tok'}, dimensions={0}, use_global_device_ids=true | all-gather | bytes 4352 | tf_op jit(solution)/shard_map/all_gather | solution.py:88
  37.4 0.0 collective-permute-done.1
  37.4 0.0 collective-permute-start.2
  37.4 0.0 copy-done.4
  37.4 11.5 %collective-permute-done.2 = bf16[64,1536]{1,0:T(8,128)(2,1)} collective-permute-done((bf16[64,1536]{1,0:T(8,128)(2,1)S(1)}, bf16[64,1536]{1,0:T(8,128)(2,1)}, u32[]{:S(2)}, u32[]{:S(2)}) %collective-permute-start.2) | collective-permute-done | bytes 196640 | tf_op jit(solution)/shard_map/ppermute | solution.py:12
  48.9 0.0 collective-permute-start.3
  48.9 0.0 copy-start.5
  48.9 6.7 %copy.26 = bf16[1536,1536]{0,1:T(8,128)(2,1)} copy(bf16[1536,1536]{1,0:T(8,128)(2,1)} %param.17) | data formatting | bytes 9437184 | tf_op args[7]
  55.6 0.0 copy-done.3
  55.7 0.1 reshape.64
  55.7 0.0 copy-done.5
  55.8 0.0 copy-start.1
  55.8 13.4 %gather_fusion = bf16[1536,1536]{1,0:T(8,128)(2,1)} fusion(bf16[1536,1536]{0,1:T(8,128)(2,1)} %copy.26, s32[2048]{0:T(1024)S(1)} %pad_clamp_fusion), kind=kCustom, calls=%fused_computation | custom fusion | bytes 9443328 | tf_op jit(solution)/shard_map/gather | solution.py:104
  69.2 0.0 copy-done.1
  69.2 8.4 %gather_fusion.1 = f32[1536]{0:T(1024)S(1)} fusion(f32[1536]{0:T(1024)S(1)} %copy-done.1, s32[2048]{0:T(1024)S(1)} %pad_clamp_fusion), kind=kCustom, calls=%fused_computation.1 | custom fusion | bytes 18432 | tf_op jit(solution)/shard_map/gather | solution.py:105
  77.5 0.0 collective-permute-done.3
  77.6 0.3 rev.3
  77.9 0.1 fusion.28
  78.1 0.1 fusion.36
  78.2 0.0 slice-done
  78.2 2.2 %fusion.10 = bf16[2,64,768]{2,1,0:T(8,128)(2,1)S(1)} fusion(bf16[1536,768]{1,0:T(8,128)(2,1)} %param.13, bf16[1,64,1536]{2,1,0:T(8,128)(2,1)S(1)} %fusion.36, bf16[1,64,1536]{2,1,0:T(8,128)(2,1)S(1)} %slice-done), kind=kOutput, calls=%fused_computation.19 | convolution fusion | flops 302284800 | bytes 2949120 | tf_op jit(solution)/shard_map/std,de->ste/dot_general | solution.py:74
  80.4 1.0 reshape.41
  81.3 2.0 %fusion.4 = (f32[2,256]{1,0:T(2,128)S(1)}, f32[2,256,1024]{2,1,0:T(8,128)S(1)}) fusion(pred[2,1024]{1,0:T(4,128)(4,1)S(1)} %bitcast.40, bf16[2,256,192]{2,1,0:T(8,128)(2,1)} %reshape.41, bf16[2,1024,384]{2,1,0:T(8,128)(2,1)} %all-gather.3.cloned.1.call-done), kind=kOutput, calls=%fused_computation.10 | convolution fusion | flops 202898944 | bytes 3411968 | tf_op jit(solution)/shard_map/srd,skd->srk/dot_general | solution.py:29
  83.4 0.6 fusion.5
  84.0 0.0 copy-done.6
  84.0 1.2 %fusion.9 = bf16[2,256,192]{1,2,0:T(8,128)(2,1)S(1)} fusion(f32[2,256,1024]{2,1,0:T(8,128)S(1)} %get-tuple-element.8, bf16[2,1024,384]{2,1,0:T(8,128)(2,1)S(1)} %copy-done.6, f32[2,256]{1,0:T(2,128)S(1)} %broadcast_maximum_fusion, pred[2,1024]{1,0:T(4,128)(4,1)S(1)} %bitcast.42, f32[2,256]{1,0:T(2,128)S(1)} %fusion.5), kind=kOutput, calls=%fused_computation.18 | convolution fusion | flops 204144640 | bytes 3350528 | tf_op jit(solution)/shard_map/srk,skd->srd/dot_general | solution.py:37
  85.2 0.1 copy.25
  85.3 0.3 reshape.42
  85.6 0.0 copy-done
  85.6 0.6 multiply_reduce_fusion
  86.2 0.2 multiply_convert_fusion
  86.4 3.4 %fusion.31 = bf16[64,1536]{1,0:T(8,128)(2,1)S(1)} fusion(bf16[1536,1536]{1,0:T(8,128)(2,1)} %param.17, bf16[2,64,1536]{2,1,0:T(8,128)(2,1)S(1)} %multiply_convert_fusion, f32[1536]{0:T(1024)S(1)} %copy-done.1), kind=kOutput, calls=%fused_computation.42 | convolution fusion | flops 302776320 | bytes 5120000 | tf_op jit(solution)/shard_map/dot_general | solution.py:101
  89.8 4.7 %add_multiply_fusion = f32[64,1536]{1,0:T(8,128)} fusion(bf16[1536,1536]{1,0:T(8,128)(2,1)} %gather_fusion, bf16[64,1536]{1,0:T(8,128)(2,1)S(1)} %fusion.31, bf16[2,64,1536]{2,1,0:T(8,128)(2,1)S(1)} %multiply_convert_fusion, f32[1536]{0:T(1024)S(1)} %gather_fusion.1), kind=kOutput, calls=%fused_computation.48 | convolution fusion | flops 303169536 | bytes 5513216 | tf_op jit(solution)/shard_map/dot_general | solution.py:104
  (15 shorter events, 0.1 us)
Async XLA Ops:
  6.5 79.1 %copy-start = (bf16[768,1536]{1,0:T(8,128)(2,1)S(1)}, bf16[768,1536]{1,0:T(8,128)(2,1)}, u32[]{:S(2)}) copy-start(bf16[768,1536]{1,0:T(8,128)(2,1)} %param.15) | copy-start | bytes 7077892
  6.5 5.7 %copy-start.2 = (bf16[2,64,1536]{2,1,0:T(8,128)(2,1)S(1)}, bf16[2,64,1536]{2,1,0:T(8,128)(2,1)}, u32[]{:S(2)}) copy-start(bf16[2,64,1536]{2,1,0:T(8,128)(2,1)} %param.10) | copy-start | bytes 1179652
  6.5 10.2 %copy-start.7 = (s32[2,64]{1,0:T(2,128)S(1)}, s32[2,64]{1,0:T(2,128)}, u32[]{:S(2)}) copy-start(s32[2,64]{1,0:T(2,128)} %param.11) | copy-start | bytes 1540
  6.5 30.9 %copy-start.4 = (s32[1536]{0:T(1024)S(1)}, s32[1536]{0:T(1024)}, u32[]{:S(2)}) copy-start(s32[1536]{0:T(1024)} %param.19) | copy-start | bytes 18436
  6.5 74.8 %all-gather.3.cloned.1.call-start = ((), (), s32[]{:S(2)}) async-start(), calls=%async_computation | async-start | bytes 1671168 | tf_op jit(solution)/shard_map/all_gather | solution.py:87
  9.8 45.9 %copy-start.3 = (bf16[2,64,1536]{2,1,0:T(8,128)(2,1)}, bf16[2,64,1536]{2,1,0:T(8,128)(2,1)S(1)}, u32[]{:S(2)}) copy-start(bf16[2,64,1536]{2,1,0:T(8,128)(2,1)S(1)} %fusion.27) | copy-start | bytes 1179652
  12.3 1.6 %collective-permute-start = (bf16[64,1536]{1,0:T(8,128)(2,1)S(1)}, bf16[64,1536]{1,0:T(8,128)(2,1)S(1)}, u32[]{:S(2)}, u32[]{:S(2)}) collective-permute-start(bf16[64,1536]{1,0:T(8,128)(2,1)S(1)} %get-tuple-element.6), channel_id=1, source_target_pairs={{0,1},{1,0},{2,3},{3,2},{4,5},{5,4},{6,7},{7,6},{8,9},{9,8},{10,11... | collective-permute-start | bytes 589832 | tf_op jit(solution)/shard_map/ppermute | solution.py:12
  13.9 23.5 %collective-permute-start.1 = (bf16[64,1536]{1,0:T(8,128)(2,1)S(1)}, bf16[64,1536]{1,0:T(8,128)(2,1)S(1)}, u32[]{:S(2)}, u32[]{:S(2)}) collective-permute-start(bf16[64,1536]{1,0:T(8,128)(2,1)S(1)} %collective-permute-done), channel_id=1, source_target_pairs={{0,2},{1,3},{2,0},{3,1},{4,6},{5,7},{6,4},{7,5},{8,10},{9,11},{10,... | collective-permute-start | bytes 589832 | tf_op jit(solution)/shard_map/ppermute | solution.py:12
  37.4 11.5 %collective-permute-start.2 = (bf16[64,1536]{1,0:T(8,128)(2,1)S(1)}, bf16[64,1536]{1,0:T(8,128)(2,1)}, u32[]{:S(2)}, u32[]{:S(2)}) collective-permute-start(bf16[64,1536]{1,0:T(8,128)(2,1)S(1)} %collective-permute-done.1), channel_id=1, source_target_pairs={{0,4},{1,5},{2,6},{3,7},{4,0},{5,1},{6,2},{7,3},{8,12},{9,13},{10,... | collective-permute-start | bytes 589832 | tf_op jit(solution)/shard_map/ppermute | solution.py:12
  48.9 28.7 %collective-permute-start.3 = (bf16[64,1536]{1,0:T(8,128)(2,1)}, bf16[64,1536]{1,0:T(8,128)(2,1)S(1)}, u32[]{:S(2)}, u32[]{:S(2)}) collective-permute-start(bf16[64,1536]{1,0:T(8,128)(2,1)} %collective-permute-done.2), channel_id=1, source_target_pairs={{0,8},{1,9},{2,10},{3,11},{4,12},{5,13},{6,14},{7,15},{8,0},{9,1},... | collective-permute-start | bytes 589832 | tf_op jit(solution)/shard_map/ppermute | solution.py:12
  48.9 6.8 %copy-start.5 = (bf16[1536]{0:T(1024)(128)(2,1)S(1)}, bf16[1536]{0:T(1024)(128)(2,1)}, u32[]{:S(2)}) copy-start(bf16[1536]{0:T(1024)(128)(2,1)} %param.16) | copy-start | bytes 9220
  55.8 13.4 %copy-start.1 = (f32[1536]{0:T(1024)S(1)}, f32[1536]{0:T(1024)}, u32[]{:S(2)}) copy-start(f32[1536]{0:T(1024)} %param.18) | copy-start | bytes 18436
  69.2 9.0 %slice-start = ((bf16[2,64,1536]{2,1,0:T(8,128)(2,1)}), bf16[1,64,1536]{2,1,0:T(8,128)(2,1)S(1)}, s32[]{:S(2)}) async-start(bf16[2,64,1536]{2,1,0:T(8,128)(2,1)} %copy-done.3), calls=%async_computation.1 | async-start | bytes 393216 | tf_op jit(solution)/shard_map/slice | solution.py:72
  81.3 2.7 %copy-start.6 = (bf16[2,1024,384]{2,1,0:T(8,128)(2,1)S(1)}, bf16[2,1024,384]{2,1,0:T(8,128)(2,1)}, u32[]{:S(2)}) copy-start(bf16[2,1024,384]{2,1,0:T(8,128)(2,1)} %all-gather.3.cloned.1.call-done) | copy-start | bytes 4718596
Sparse Core Ops, SparseCore 0:
  12.3 45.7 all-gather.2
where the time goes:
time: 102 us; the launch traced here: 101 us
  local copies, waits for them, and re-layouts  30.3 us (30%)
  blocking collectives  20.7 us (20%)
  matrix products  16.5 us (16%)
  between operations  13.6 us (13%)
  waiting for transfers between devices  12.6 us (12%)
  other arithmetic  4.27 us (4%)
  starting transfers between devices  3.44 us (3%)
    all_gather x1, blocking collectives, per_device(): lax.all_gather(usable_flag, 'tok', axis=1, tiled=True)  20.7 us
    gather x1, local copies, waits for them, and re-layouts, per_device(): head_weight[:, track_perm]  13.4 us
    ppermute x4, waiting for transfers between devices, swapped(): return lax.ppermute(value, axis, pairs)  12.5 us
    gather x1, local copies, waits for them, and re-layouts, per_device(): head_bias[track_perm]  8.38 us
    unnamed x17, local copies, waits for them, and re-layouts  6.77 us
    dot_general x1, matrix products, per_device(): jnp.dot(normed_out[1], head_weight[:, track_perm], preferred_element_type...  4.69 us
    dot_general x1, matrix products, per_device(): jnp.dot(normed_out[0], head_weight, preferred_element_type=jnp.float32)  3.42 us
    ppermute x4, starting transfers between devices, swapped(): return lax.ppermute(value, axis, pairs)  3.41 us
  transfers between devices with their start and end apart: 5, of which 2 were waited for; matrix products, arithmetic and copies ran while one was open for 32% of the time, Pallas kernels for 0%

commit v1 on v0

v1 whole, which is shorter than its diff:
```python
import functools
import math

import jax
import jax.numpy as jnp
from jax import lax
from jax.experimental import pallas as pl
from jax.experimental.pallas import tpu as pltpu
from jax.sharding import PartitionSpec as P

VMEM = pl.BlockSpec(memory_space=pltpu.VMEM)
SMEM = pl.BlockSpec(memory_space=pltpu.SMEM)
ANY = pl.BlockSpec(memory_space=pl.ANY)
F32 = jnp.float32
BF16 = jnp.bfloat16


def exchange(value, mask):
    count = lax.axis_size("tok")
    return lax.ppermute(value, "tok", [(s, s ^ mask) for s in range(count)])


def normalize(rows, gain):
    mean = jnp.mean(rows * rows, -1, keepdims=True)
    return (rows * lax.rsqrt(mean + 1e-06) * gain).astype(BF16)


def project_kernel(core_ref, own_ref, got_ref, own_ids_ref, got_ids_ref, gain_ref, weight_ref, kv_ref, rows_ref):
    core = core_ref[0]
    tokens = own_ref.shape[1]
    head = weight_ref.shape[1] // 2
    gain = gain_ref[...].astype(F32)
    row = lax.broadcasted_iota(jnp.int32, (tokens, tokens), 0)
    col = lax.broadcasted_iota(jnp.int32, (tokens, tokens), 1)
    source = jnp.where(core == 0, row, tokens - 1 - row)
    turn = jnp.where(col == source, 1.0, 0.0).astype(BF16)
    lane = lax.broadcasted_iota(jnp.int32, (tokens, weight_ref.shape[1]), 1)
    normed = []
    hidden_flags = []
    for part, (ref, ids_ref) in enumerate(((own_ref, own_ids_ref), (got_ref, got_ids_ref))):
        block = ref[core]
        ids = jnp.where(core == 0, ids_ref[0:1, :], ids_ref[1:2, :])
        unknown = jnp.where((row == col) & (ids == 4), 1.0, 0.0)
        hidden_flags.append(jnp.max(unknown, -1, keepdims=True))
        normed.append(normalize(block.astype(F32), gain))
        rows_ref[pl.ds(part * tokens, tokens), :] = jnp.dot(
            turn, block, preferred_element_type=F32
        ).astype(BF16)
    kv = jnp.dot(jnp.concatenate(normed, 0), weight_ref[...], preferred_element_type=F32)
    for part in range(2):
        left_out = (lane < head) & (hidden_flags[part] > 0.5)
        kv_ref[pl.ds(part * tokens, tokens), :] = jnp.where(
            left_out, jnp.nan, kv[part * tokens : (part + 1) * tokens]
        ).astype(BF16)


def project(core, own, got, own_ids, got_ids, gain, weight):
    tokens, width = own.shape[1:]
    return pl.pallas_call(
        project_kernel,
        out_shape=(
            jax.ShapeDtypeStruct((2 * tokens, weight.shape[1]), BF16),
            jax.ShapeDtypeStruct((2 * tokens, width), BF16),
        ),
        in_specs=[SMEM] + [VMEM] * 6,
        out_specs=(VMEM, VMEM),
        compiler_params=pltpu.CompilerParams(vmem_limit_bytes=16 << 20),
        cost_estimate=pl.CostEstimate(
            flops=4 * tokens * width * weight.shape[1], bytes_accessed=2 * weight.size, transcendentals=0
        ),
        name="project",
    )(core, own, got, own_ids, got_ids, gain, weight)


def block_kernel(count, heads, core_ref, rows_ref, *refs):
    kv_refs = refs[:count]
    (gain_ref, head_gain_ref, bias_ref, wq_hbm, wo_hbm, wh_hbm, keep_ref, send_ref) = refs[count : count + 8]
    wq, wo, wh, kv, queries, attended, predictions, sems = refs[count + 8 :]
    copies = [
        pltpu.make_async_copy(wq_hbm, wq, sems.at[0]),
        pltpu.make_async_copy(wo_hbm, wo, sems.at[1]),
        pltpu.make_async_copy(wh_hbm, wh, sems.at[2]),
    ]
    for copy in copies:
        copy.start()
    core = core_ref[0]
    head = kv.shape[1] // 2
    tokens = rows_ref.shape[0]
    start = 0
    for ref in kv_refs:
        kv[pl.ds(start, ref.shape[0]), :] = ref[...]
        start += ref.shape[0]
    length = start
    rows = rows_ref[...].astype(F32)
    normed = normalize(rows, gain_ref[...].astype(F32))
    copies[0].wait()
    queries[...] = jnp.dot(normed, wq[...], preferred_element_type=F32).astype(BF16)
    scale = 1.0 / math.sqrt(head)
    chunk = min(length, 1024)
    for number in range(heads):
        query = queries[:, number * head : (number + 1) * head]

        def step(position, state):
            maxima, totals, summed = state
            at = pl.multiple_of(position * chunk, chunk)
            part = kv[pl.ds(at, chunk), :]
            scores = lax.dot_general(
                query, part[:, :head], (((1,), (1,)), ((), ())), preferred_element_type=F32
            )
            scores = jnp.where(scores == scores, scores * scale, -1e30)
            higher = jnp.maximum(maxima, jnp.max(scores, -1, keepdims=True))
            weights = jnp.exp(scores - higher)
            kept = jnp.exp(maxima - higher)
            totals = totals * kept + jnp.sum(weights, -1, keepdims=True)
            summed = summed * kept + jnp.dot(
                weights.astype(BF16), part[:, head:], preferred_element_type=F32
            )
            return higher, totals, summed

        state = (
            jnp.full((tokens, 1), -1e30, F32),
            jnp.zeros((tokens, 1), F32),
            jnp.zeros((tokens, head), F32),
        )
        if length == chunk:
            state = step(0, state)
        else:
            state = lax.fori_loop(0, length // chunk, step, state)
        attended[:, number * head : (number + 1) * head] = (state[2] / state[1]).astype(BF16)
    copies[1].wait()
    summed = rows + jnp.dot(attended[...], wo[...], preferred_element_type=F32)
    normed_out = normalize(summed, head_gain_ref[...].astype(F32))
    copies[2].wait()
    tracks = wh.shape[1]
    width = 256
    for at in range(0, tracks, width):
        logits = jnp.dot(normed_out, wh[:, at : at + width], preferred_element_type=F32)
        logits = logits + bias_ref[:, at : at + width]
        soft = jnp.maximum(logits, 0.0) + jnp.log1p(jnp.exp(-jnp.abs(logits)))
        predictions[:, at : at + width] = soft.astype(BF16)
    half = tokens // 2
    keep_ref[...] = predictions[pl.ds(pl.multiple_of(core * half, half), half), :]
    send_ref[...] = predictions[pl.ds(pl.multiple_of((1 - core) * half, half), half), :]


def transform(core, rows, kvs, gain, head_gain, bias, wq, wo, wh):
    tokens, width = rows.shape
    head = kvs[0].shape[1] // 2
    heads = wq.shape[1] // head
    length = sum(kv.shape[0] for kv in kvs)
    tracks = wh.shape[1]
    flops = 2 * tokens * (width * wq.shape[1] * 2 + width * tracks + 2 * length * wq.shape[1])
    return pl.pallas_call(
        functools.partial(block_kernel, len(kvs), heads),
        out_shape=(jax.ShapeDtypeStruct((tokens // 2, tracks), BF16),) * 2,
        in_specs=[SMEM] + [VMEM] * (4 + len(kvs)) + [ANY] * 3,
        out_specs=(VMEM, VMEM),
        scratch_shapes=[
            pltpu.VMEM(wq.shape, BF16),
            pltpu.VMEM(wo.shape, BF16),
            pltpu.VMEM(wh.shape, BF16),
            pltpu.VMEM((length, 2 * head), BF16),
            pltpu.VMEM((tokens, heads * head), BF16),
            pltpu.VMEM((tokens, heads * head), BF16),
            pltpu.VMEM((tokens, tracks), BF16),
            pltpu.SemaphoreType.DMA((3,)),
        ],
        compiler_params=pltpu.CompilerParams(vmem_limit_bytes=40 << 20),
        cost_estimate=pl.CostEstimate(
            flops=flops, bytes_accessed=2 * (wq.size + wo.size + wh.size), transcendentals=tokens * length * heads
        ),
        name="transform",
    )(core, rows, *kvs, gain, head_gain, bias, wq, wo, wh)


def combine_kernel(core_ref, keep_ref, got_ref, perm_ref, out_ref):
    forward_here = core_ref[0] == 0
    tracks = perm_ref.shape[1]
    tokens = keep_ref.shape[0]
    lanes = 128
    keep = keep_ref[...].astype(F32)
    got = got_ref[...].astype(F32)
    forward = jnp.where(forward_here, keep, got)
    reverse = jnp.where(forward_here, got, keep)
    for at in range(0, tracks, lanes):
        perm = jnp.broadcast_to(perm_ref[:, at : at + lanes], (tokens, lanes))
        within = perm & (lanes - 1)
        tile = perm >> 7
        picked = jnp.zeros((tokens, lanes), F32)
        for number in range(tracks // lanes):
            source = reverse[:, number * lanes : (number + 1) * lanes]
            found = jnp.take_along_axis(source, within, axis=1)
            picked = jnp.where(tile == number, found, picked)
        out_ref[:, at : at + lanes] = 0.5 * (forward[:, at : at + lanes] + picked)


def combine(core, keep, got, perm):
    return pl.pallas_call(
        combine_kernel,
        out_shape=jax.ShapeDtypeStruct(keep.shape, F32),
        in_specs=[SMEM] + [VMEM] * 3,
        out_specs=VMEM,
        compiler_params=pltpu.CompilerParams(vmem_limit_bytes=16 << 20),
        name="combine",
    )(core, keep, got, perm)


def gathered(kv):
    count = lax.axis_size("tok")
    if count > 16:
        mask = 2
        while mask < count:
            kv = jnp.concatenate([kv, exchange(kv, mask)], 0)
            mask *= 2
        return [kv]
    blocks = [kv] + [exchange(kv, mask) for mask in range(4, count, 4)]
    if count > 2:
        blocks += [exchange(block, 2) for block in blocks]
    return blocks


def per_device(
    hidden,
    base_ids,
    attn_gain,
    q_weight,
    kv_weight,
    out_weight,
    head_gain,
    head_weight,
    head_bias,
    track_perm,
):
    count = lax.axis_size("tok")
    core = (lax.axis_index("tok") % 2).astype(jnp.int32).reshape(1)
    got = exchange(hidden, 1)
    got_ids = exchange(base_ids, 1)
    gain = attn_gain.reshape(1, -1)
    kv, rows = project(core, hidden, got, base_ids, got_ids, gain, kv_weight)
    rows = lax.ppermute(
        rows, "tok", [(s, s if s % 2 == 0 else count - s) for s in range(count)]
    )
    keep, send = transform(
        core,
        rows,
        gathered(kv),
        gain,
        head_gain.reshape(1, -1),
        head_bias.reshape(1, -1),
        q_weight,
        out_weight,
        head_weight,
    )
    return combine(core, keep, exchange(send, 1), track_perm.reshape(1, -1))


def solution(mesh):
    placed = (P("grp", "tok", None), P("grp", "tok"), P(), P(), P(), P(), P(), P(), P(), P())
    return jax.shard_map(
        per_device, mesh=mesh, in_specs=placed, out_specs=P(("grp", "tok"), None), check_vma=False
    )
```

time: 102 us -> 47.4 us (0.46)
  blocking collectives: 20.7 us -> 0 us
  local copies, waits for them, and re-layouts: 30.3 us -> 10.7 us
  matrix products: 16.5 us -> 0 us
  between operations: 13.6 us -> 0.05 us
  starting transfers between devices: 3.44 us -> 14.4 us
  Pallas kernels: 0 us -> 7.03 us
  other arithmetic: 4.27 us -> 0 us
  waiting for transfers between devices: 12.6 us -> 14.8 us
    gather x2 -> x0, local copies, waits for them, and re-layouts: 21.7 us -> none  [the longest x1 13.4 us: per_device(): head_weight[:, track_perm]]
    all_gather x1 -> x0, blocking collectives: 20.7 us -> none  [per_device(): lax.all_gather(usable_flag, 'tok', axis=1, tiled=True)]
    dot_general x7 -> x0, matrix products: 16.5 us -> none  [the longest x1 4.69 us: per_device(): jnp.dot(normed_out[1], head_weight[:, track_perm], preferred_element_type...]
    ppermute x4 -> x11, starting transfers between devices: 3.41 us -> 14.4 us  [the longest x10 13.7 us: exchange(): return lax.ppermute(value, 'tok', [(s, s ^ mask) for s in range(count)])]
    pallas_call x0 -> x3, Pallas kernels: none -> 7.03 us  [the longest x1 5.02 us: transform(): pl.pallas_call(functools.partial(block_kernel, len(kvs), heads), out_shap...]
    ppermute x4 -> x11, waiting for transfers between devices: 12.5 us -> 14.8 us  [the longest x10 14.8 us: exchange(): return lax.ppermute(value, 'tok', [(s, s ^ mask) for s in range(count)])]
    convert_element_type x4 -> x0, other arithmetic: 2.16 us -> none  [the longest x1 1.16 us: per_device(): normed = normalize(hidden, attn_gain).astype(jnp.bfloat16)]
    reduce_sum x3 -> x0, other arithmetic: 1.92 us -> none  [the longest x2 1.29 us: normalize(): jnp.mean(widened * widened, -1, keepdims=True) + 1e-06]
  transfers between devices with their start and end apart: 5 -> 11, of which waited for: 2 -> 5; matrix products, arithmetic and copies ran while one was open for 32% -> 4% of each run, Pallas kernels for 0% -> 0%
where the time goes in v1:
time: 47.4 us; the launch traced here: 47 us
  waiting for transfers between devices  14.8 us (31%)
  starting transfers between devices  14.4 us (30%)
  local copies, waits for them, and re-layouts  10.7 us (23%)
  Pallas kernels  7.03 us (15%)
    ppermute x10, waiting for transfers between devices, exchange(): return lax.ppermute(value, 'tok', [(s, s ^ mask) for s in range(count)])  14.8 us
    ppermute x10, starting transfers between devices, exchange(): return lax.ppermute(value, 'tok', [(s, s ^ mask) for s in range(count)])  13.7 us
    unnamed x14, local copies, waits for them, and re-layouts  8.62 us
    pallas_call x1, Pallas kernels, transform(): pl.pallas_call(functools.partial(block_kernel, len(kvs), heads), out_shap...  5.02 us
    pallas_call x1, Pallas kernels, combine(): pl.pallas_call(combine_kernel, out_shape=jax.ShapeDtypeStruct(keep.shape,...  1.47 us
  transfers between devices with their start and end apart: 11, of which 5 were waited for; matrix products, arithmetic and copies ran while one was open for 4% of the time, Pallas kernels for 0%

profile of v1, /device:TPU:0, one launch (start us, length us, event | category | flops | bytes accessed | tf_op | source)
XLA Modules:
  0.0 47.0 jit_solution(11503601887044433966)
XLA Ops:
  0.0 0.5 %collective-permute-start = (bf16[2,64,1536]{2,1,0:T(8,128)(2,1)}, bf16[2,64,1536]{2,1,0:T(8,128)(2,1)S(1)}, u32[]{:S(2)}, u32[]{:S(2)}) collective-permute-start(bf16[2,64,1536]{2,1,0:T(8,128)(2,1)} %own_ref.1), channel_id=1, source_target_pairs={{0,1},{1,0},{2,3},{3,2},{4,5},{5,4},{6,7},{7,6},{8,9},{9,8},{10,11... | collective-permute-start | bytes 1179656 | tf_op jit(solution)/shard_map/ppermute | solution.py:20
  0.5 0.0 collective-permute-start.1
  0.5 0.7 %reshape.16.gain_ref.refs_8_ = bf16[1,1536]{1,0:T(2,128)(2,1)S(1)} reshape(bf16[1536]{0:T(1024)(128)(2,1)} %param.12) | data formatting | bytes 6144 | tf_op jit(solution)/shard_map/reshape | solution.py:238
  1.2 0.9 %collective-permute-done.1.got_ids_ref = s32[2,64]{1,0:T(2,128)S(1)} collective-permute-done((s32[2,64]{1,0:T(2,128)}, s32[2,64]{1,0:T(2,128)S(1)}, u32[]{:S(2)}, u32[]{:S(2)}) %collective-permute-start.1) | collective-permute-done | bytes 544 | tf_op jit(solution)/shard_map/ppermute | solution.py:20
  2.1 0.0 collective-permute-done.got_ref
  2.1 0.0 copy-start.3
  2.1 1.3 %copy-done.3 = bf16[1536,384]{1,0:T(8,128)(2,1)S(1)} copy-done((bf16[1536,384]{1,0:T(8,128)(2,1)S(1)}, bf16[1536,384]{1,0:T(8,128)(2,1)}, u32[]{:S(2)}) %copy-start.3) | copy-done | bytes 1179672
  3.3 0.0 copy-start.4
  3.3 1.0 %copy-done.4 = bf16[2,64,1536]{2,1,0:T(8,128)(2,1)S(1)} copy-done((bf16[2,64,1536]{2,1,0:T(8,128)(2,1)S(1)}, bf16[2,64,1536]{2,1,0:T(8,128)(2,1)}, u32[]{:S(2)}) %copy-start.4) | copy-done | bytes 393240
  4.3 0.0 copy-start.5
  4.3 0.7 %copy-done.5 = s32[2,64]{1,0:T(2,128)S(1)} copy-done((s32[2,64]{1,0:T(2,128)S(1)}, s32[2,64]{1,0:T(2,128)}, u32[]{:S(2)}) %copy-start.5) | copy-done | bytes 536
  5.0 0.5 %project.1 = (bf16[128,384]{1,0:T(8,128)(2,1)S(1)}, bf16[128,1536]{1,0:T(8,128)(2,1)S(1)}) custom-call(s32[1]{0:T(128)} %bitcast.core_ref, bf16[2,64,1536]{2,1,0:T(8,128)(2,1)S(1)} %copy-done.4, bf16[2,64,1536]{2,1,0:T(8,128)(2,1)S(1)} %collective-permute-done.got_ref, s32[2,64]{1,0:T(2,128)S(1)} %copy-done.5, ...), custom_call_target="tpu_custom_call" | custom-call | flops 150994944 | bytes 1179648 | tf_op jit(solution)/shard_map/project/pallas_call | solution.py:59
  5.5 0.7 %collective-permute-start.2 = (bf16[128,1536]{1,0:T(8,128)(2,1)S(1)}, bf16[128,1536]{1,0:T(8,128)(2,1)S(1)}, u32[]{:S(2)}, u32[]{:S(2)}) collective-permute-start(bf16[128,1536]{1,0:T(8,128)(2,1)S(1)} %get-tuple-element.9), channel_id=1, source_target_pairs={{0,0},{1,15},{2,2},{3,13},{4,4},{5,11},{6,6},{7,9},{8,8},{9,7},{10... | collective-permute-start | bytes 1179656 | tf_op jit(solution)/shard_map/ppermute | solution.py:240
  6.2 3.0 %collective-permute-start.3 = (bf16[128,384]{1,0:T(8,128)(2,1)S(1)}, bf16[128,384]{1,0:T(8,128)(2,1)S(1)}, u32[]{:S(2)}, u32[]{:S(2)}) collective-permute-start(bf16[128,384]{1,0:T(8,128)(2,1)S(1)} %get-tuple-element.10.refs_0_), channel_id=1, source_target_pairs={{0,4},{1,5},{2,6},{3,7},{4,0},{5,1},{6,2},{7,3},{8,12},{9,13},{10,... | collective-permute-start | bytes 294920 | tf_op jit(solution)/shard_map/ppermute | solution.py:20
  9.2 2.6 %collective-permute-start.4 = (bf16[128,384]{1,0:T(8,128)(2,1)S(1)}, bf16[128,384]{1,0:T(8,128)(2,1)S(1)}, u32[]{:S(2)}, u32[]{:S(2)}) collective-permute-start(bf16[128,384]{1,0:T(8,128)(2,1)S(1)} %get-tuple-element.10.refs_0_), channel_id=1, source_target_pairs={{0,8},{1,9},{2,10},{3,11},{4,12},{5,13},{6,14},{7,15},{8,0},{9,1},... | collective-permute-start | bytes 294920 | tf_op jit(solution)/shard_map/ppermute | solution.py:20
  11.8 0.0 collective-permute-start.5
  11.8 1.7 %collective-permute-start.6 = (bf16[128,384]{1,0:T(8,128)(2,1)S(1)}, bf16[128,384]{1,0:T(8,128)(2,1)S(1)}, u32[]{:S(2)}, u32[]{:S(2)}) collective-permute-start(bf16[128,384]{1,0:T(8,128)(2,1)S(1)} %get-tuple-element.10.refs_0_), channel_id=1, source_target_pairs={{0,2},{1,3},{2,0},{3,1},{4,6},{5,7},{6,4},{7,5},{8,10},{9,11},{10,... | collective-permute-start | bytes 294920 | tf_op jit(solution)/shard_map/ppermute | solution.py:20
  13.5 0.0 collective-permute-done.3.refs_1_
  13.5 0.3 collective-permute-start.7
  13.9 10.4 %collective-permute-done.4.refs_2_ = bf16[128,384]{1,0:T(8,128)(2,1)S(1)} collective-permute-done((bf16[128,384]{1,0:T(8,128)(2,1)S(1)}, bf16[128,384]{1,0:T(8,128)(2,1)S(1)}, u32[]{:S(2)}, u32[]{:S(2)}) %collective-permute-start.4) | collective-permute-done | bytes 98336 | tf_op jit(solution)/shard_map/ppermute | solution.py:20
  24.3 1.3 %collective-permute-start.8 = (bf16[128,384]{1,0:T(8,128)(2,1)S(1)}, bf16[128,384]{1,0:T(8,128)(2,1)S(1)}, u32[]{:S(2)}, u32[]{:S(2)}) collective-permute-start(bf16[128,384]{1,0:T(8,128)(2,1)S(1)} %collective-permute-done.4.refs_2_), channel_id=1, source_target_pairs={{0,2},{1,3},{2,0},{3,1},{4,6},{5,7},{6,4},{7,5},{8,10},{9,11},{10,... | collective-permute-start | bytes 294920 | tf_op jit(solution)/shard_map/ppermute | solution.py:20
  25.6 0.0 collective-permute-done.5.refs_3_
  25.6 0.7 %collective-permute-start.9 = (bf16[128,384]{1,0:T(8,128)(2,1)S(1)}, bf16[128,384]{1,0:T(8,128)(2,1)S(1)}, u32[]{:S(2)}, u32[]{:S(2)}) collective-permute-start(bf16[128,384]{1,0:T(8,128)(2,1)S(1)} %collective-permute-done.5.refs_3_), channel_id=1, source_target_pairs={{0,2},{1,3},{2,0},{3,1},{4,6},{5,7},{6,4},{7,5},{8,10},{9,11},{10,... | collective-permute-start | bytes 294920 | tf_op jit(solution)/shard_map/ppermute | solution.py:20
  26.3 0.7 %reshape.17.refs_9_ = bf16[1,1536]{1,0:T(2,128)(2,1)S(1)} reshape(bf16[1536]{0:T(1024)(128)(2,1)} %param.16) | data formatting | bytes 6144 | tf_op jit(solution)/shard_map/reshape | solution.py:248
  27.0 0.0 copy-start.6
  27.0 0.7 %reshape.18.refs_10_ = f32[1,1536]{1,0:T(1,128)S(1)} reshape(f32[1536]{0:T(1024)} %param.18) | data formatting | bytes 12288 | tf_op jit(solution)/shard_map/reshape | solution.py:249
  27.7 0.0 collective-permute-done.6.refs_4_
  27.7 0.0 collective-permute-done.7.refs_5_
  27.7 1.2 %collective-permute-done.8.refs_6_ = bf16[128,384]{1,0:T(8,128)(2,1)S(1)} collective-permute-done((bf16[128,384]{1,0:T(8,128)(2,1)S(1)}, bf16[128,384]{1,0:T(8,128)(2,1)S(1)}, u32[]{:S(2)}, u32[]{:S(2)}) %collective-permute-start.8) | collective-permute-done | bytes 98336 | tf_op jit(solution)/shard_map/ppermute | solution.py:20
  28.9 1.3 %collective-permute-done.9.refs_7_ = bf16[128,384]{1,0:T(8,128)(2,1)S(1)} collective-permute-done((bf16[128,384]{1,0:T(8,128)(2,1)S(1)}, bf16[128,384]{1,0:T(8,128)(2,1)S(1)}, u32[]{:S(2)}, u32[]{:S(2)}) %collective-permute-start.9) | collective-permute-done | bytes 98336 | tf_op jit(solution)/shard_map/ppermute | solution.py:20
  30.2 0.0 collective-permute-done.2.rows_ref
  30.2 0.0 copy-start
  30.2 2.3 %copy-done = bf16[1536,1536]{1,0:T(8,128)(2,1)S(1)} copy-done((bf16[1536,1536]{1,0:T(8,128)(2,1)S(1)}, bf16[1536,1536]{1,0:T(8,128)(2,1)}, u32[]{:S(2)}) %copy-start) | copy-done | bytes 4718616
  32.5 0.0 copy-start.1
  32.5 1.7 %copy-done.1 = bf16[1536,768]{1,0:T(8,128)(2,1)S(1)} copy-done((bf16[1536,768]{1,0:T(8,128)(2,1)S(1)}, bf16[1536,768]{1,0:T(8,128)(2,1)}, u32[]{:S(2)}) %copy-start.1) | copy-done | bytes 2359320
  34.2 0.0 copy-start.2
  34.2 1.7 %copy-done.2 = bf16[768,1536]{1,0:T(8,128)(2,1)S(1)} copy-done((bf16[768,1536]{1,0:T(8,128)(2,1)S(1)}, bf16[768,1536]{1,0:T(8,128)(2,1)}, u32[]{:S(2)}) %copy-start.2) | copy-done | bytes 2359320
  35.9 5.0 %transform.1 = (bf16[64,1536]{1,0:T(8,128)(2,1)S(1)}, bf16[64,1536]{1,0:T(8,128)(2,1)S(1)}) custom-call(s32[1]{0:T(128)} %bitcast.core_ref, bf16[128,1536]{1,0:T(8,128)(2,1)S(1)} %collective-permute-done.2.rows_ref, bf16[128,384]{1,0:T(8,128)(2,1)S(1)} %get-tuple-element.10.refs_0_, bf16[128,384]{1,0:T(8,128)(2,1)S(1)} %collective-permute-done.3.refs_1_, ...), custom_call_target="tpu_custom_call" | custom-call | flops 1610612736 | bytes 9437184 | tf_op jit(solution)/shard_map/transform/pallas_call | solution.py:153
  40.9 3.6 %collective-permute-start.10 = (bf16[64,1536]{1,0:T(8,128)(2,1)S(1)}, bf16[64,1536]{1,0:T(8,128)(2,1)S(1)}, u32[]{:S(2)}, u32[]{:S(2)}) collective-permute-start(bf16[64,1536]{1,0:T(8,128)(2,1)S(1)} %get-tuple-element.12), channel_id=1, source_target_pairs={{0,1},{1,0},{2,3},{3,2},{4,5},{5,4},{6,7},{7,6},{8,9},{9,8},{10,11... | collective-permute-start | bytes 589832 | tf_op jit(solution)/shard_map/ppermute | solution.py:20
  44.5 0.0 copy-done.6
  44.5 1.1 %collective-permute-done.10.got_ref = bf16[64,1536]{1,0:T(8,128)(2,1)S(1)} collective-permute-done((bf16[64,1536]{1,0:T(8,128)(2,1)S(1)}, bf16[64,1536]{1,0:T(8,128)(2,1)S(1)}, u32[]{:S(2)}, u32[]{:S(2)}) %collective-permute-start.10) | collective-permute-done | bytes 196640 | tf_op jit(solution)/shard_map/ppermute | solution.py:20
  45.5 1.5 %combine.1 = f32[64,1536]{1,0:T(8,128)} custom-call(s32[1]{0:T(128)} %bitcast.core_ref, bf16[64,1536]{1,0:T(8,128)(2,1)S(1)} %get-tuple-element.11.keep_ref, bf16[64,1536]{1,0:T(8,128)(2,1)S(1)} %collective-permute-done.10.got_ref, s32[1,1536]{1,0:T(1,128)S(1)} %reshape.19.perm_ref), custom_call_target="tpu_custom_call" | custom-call | tf_op jit(solution)/shard_map/combine/pallas_call | solution.py:198
  (1 shorter events, 0.0 us)
Async XLA Ops:
  0.0 2.1 %collective-permute-start = (bf16[2,64,1536]{2,1,0:T(8,128)(2,1)}, bf16[2,64,1536]{2,1,0:T(8,128)(2,1)S(1)}, u32[]{:S(2)}, u32[]{:S(2)}) collective-permute-start(bf16[2,64,1536]{2,1,0:T(8,128)(2,1)} %own_ref.1), channel_id=1, source_target_pairs={{0,1},{1,0},{2,3},{3,2},{4,5},{5,4},{6,7},{7,6},{8,9},{9,8},{10,11... | collective-permute-start | bytes 1179656 | tf_op jit(solution)/shard_map/ppermute | solution.py:20
  0.5 1.6 %collective-permute-start.1 = (s32[2,64]{1,0:T(2,128)}, s32[2,64]{1,0:T(2,128)S(1)}, u32[]{:S(2)}, u32[]{:S(2)}) collective-permute-start(s32[2,64]{1,0:T(2,128)} %own_ids_ref.1), channel_id=1, source_target_pairs={{0,1},{1,0},{2,3},{3,2},{4,5},{5,4},{6,7},{7,6},{8,9},{9,8},{10,11... | collective-permute-start | bytes 1544 | tf_op jit(solution)/shard_map/ppermute | solution.py:20
  2.1 1.3 %copy-start.3 = (bf16[1536,384]{1,0:T(8,128)(2,1)S(1)}, bf16[1536,384]{1,0:T(8,128)(2,1)}, u32[]{:S(2)}) copy-start(bf16[1536,384]{1,0:T(8,128)(2,1)} %weight_ref.1) | copy-start | bytes 3538948
  3.3 1.0 %copy-start.4 = (bf16[2,64,1536]{2,1,0:T(8,128)(2,1)S(1)}, bf16[2,64,1536]{2,1,0:T(8,128)(2,1)}, u32[]{:S(2)}) copy-start(bf16[2,64,1536]{2,1,0:T(8,128)(2,1)} %own_ref.1) | copy-start | bytes 1179652
  4.3 0.7 %copy-start.5 = (s32[2,64]{1,0:T(2,128)S(1)}, s32[2,64]{1,0:T(2,128)}, u32[]{:S(2)}) copy-start(s32[2,64]{1,0:T(2,128)} %own_ids_ref.1) | copy-start | bytes 1540
  5.5 24.6 %collective-permute-start.2 = (bf16[128,1536]{1,0:T(8,128)(2,1)S(1)}, bf16[128,1536]{1,0:T(8,128)(2,1)S(1)}, u32[]{:S(2)}, u32[]{:S(2)}) collective-permute-start(bf16[128,1536]{1,0:T(8,128)(2,1)S(1)} %get-tuple-element.9), channel_id=1, source_target_pairs={{0,0},{1,15},{2,2},{3,13},{4,4},{5,11},{6,6},{7,9},{8,8},{9,7},{10... | collective-permute-start | bytes 1179656 | tf_op jit(solution)/shard_map/ppermute | solution.py:240
  6.2 7.3 %collective-permute-start.3 = (bf16[128,384]{1,0:T(8,128)(2,1)S(1)}, bf16[128,384]{1,0:T(8,128)(2,1)S(1)}, u32[]{:S(2)}, u32[]{:S(2)}) collective-permute-start(bf16[128,384]{1,0:T(8,128)(2,1)S(1)} %get-tuple-element.10.refs_0_), channel_id=1, source_target_pairs={{0,4},{1,5},{2,6},{3,7},{4,0},{5,1},{6,2},{7,3},{8,12},{9,13},{10,... | collective-permute-start | bytes 294920 | tf_op jit(solution)/shard_map/ppermute | solution.py:20
  9.2 15.0 %collective-permute-start.4 = (bf16[128,384]{1,0:T(8,128)(2,1)S(1)}, bf16[128,384]{1,0:T(8,128)(2,1)S(1)}, u32[]{:S(2)}, u32[]{:S(2)}) collective-permute-start(bf16[128,384]{1,0:T(8,128)(2,1)S(1)} %get-tuple-element.10.refs_0_), channel_id=1, source_target_pairs={{0,8},{1,9},{2,10},{3,11},{4,12},{5,13},{6,14},{7,15},{8,0},{9,1},... | collective-permute-start | bytes 294920 | tf_op jit(solution)/shard_map/ppermute | solution.py:20
  11.8 13.7 %collective-permute-start.5 = (bf16[128,384]{1,0:T(8,128)(2,1)S(1)}, bf16[128,384]{1,0:T(8,128)(2,1)S(1)}, u32[]{:S(2)}, u32[]{:S(2)}) collective-permute-start(bf16[128,384]{1,0:T(8,128)(2,1)S(1)} %get-tuple-element.10.refs_0_), channel_id=1, source_target_pairs={{0,12},{1,13},{2,14},{3,15},{4,8},{5,9},{6,10},{7,11},{8,4},{9,5},... | collective-permute-start | bytes 294920 | tf_op jit(solution)/shard_map/ppermute | solution.py:20
  11.8 15.9 %collective-permute-start.6 = (bf16[128,384]{1,0:T(8,128)(2,1)S(1)}, bf16[128,384]{1,0:T(8,128)(2,1)S(1)}, u32[]{:S(2)}, u32[]{:S(2)}) collective-permute-start(bf16[128,384]{1,0:T(8,128)(2,1)S(1)} %get-tuple-element.10.refs_0_), channel_id=1, source_target_pairs={{0,2},{1,3},{2,0},{3,1},{4,6},{5,7},{6,4},{7,5},{8,10},{9,11},{10,... | collective-permute-start | bytes 294920 | tf_op jit(solution)/shard_map/ppermute | solution.py:20
  13.5 14.2 %collective-permute-start.7 = (bf16[128,384]{1,0:T(8,128)(2,1)S(1)}, bf16[128,384]{1,0:T(8,128)(2,1)S(1)}, u32[]{:S(2)}, u32[]{:S(2)}) collective-permute-start(bf16[128,384]{1,0:T(8,128)(2,1)S(1)} %collective-permute-done.3.refs_1_), channel_id=1, source_target_pairs={{0,2},{1,3},{2,0},{3,1},{4,6},{5,7},{6,4},{7,5},{8,10},{9,11},{10,... | collective-permute-start | bytes 294920 | tf_op jit(solution)/shard_map/ppermute | solution.py:20
  24.3 4.6 %collective-permute-start.8 = (bf16[128,384]{1,0:T(8,128)(2,1)S(1)}, bf16[128,384]{1,0:T(8,128)(2,1)S(1)}, u32[]{:S(2)}, u32[]{:S(2)}) collective-permute-start(bf16[128,384]{1,0:T(8,128)(2,1)S(1)} %collective-permute-done.4.refs_2_), channel_id=1, source_target_pairs={{0,2},{1,3},{2,0},{3,1},{4,6},{5,7},{6,4},{7,5},{8,10},{9,11},{10,... | collective-permute-start | bytes 294920 | tf_op jit(solution)/shard_map/ppermute | solution.py:20
  25.6 4.6 %collective-permute-start.9 = (bf16[128,384]{1,0:T(8,128)(2,1)S(1)}, bf16[128,384]{1,0:T(8,128)(2,1)S(1)}, u32[]{:S(2)}, u32[]{:S(2)}) collective-permute-start(bf16[128,384]{1,0:T(8,128)(2,1)S(1)} %collective-permute-done.5.refs_3_), channel_id=1, source_target_pairs={{0,2},{1,3},{2,0},{3,1},{4,6},{5,7},{6,4},{7,5},{8,10},{9,11},{10,... | collective-permute-start | bytes 294920 | tf_op jit(solution)/shard_map/ppermute | solution.py:20
  27.0 17.5 %copy-start.6 = (s32[1536]{0:T(1024)S(1)}, s32[1536]{0:T(1024)}, u32[]{:S(2)}) copy-start(s32[1536]{0:T(1024)} %param.19) | copy-start | bytes 18436
  30.2 2.3 %copy-start = (bf16[1536,1536]{1,0:T(8,128)(2,1)S(1)}, bf16[1536,1536]{1,0:T(8,128)(2,1)}, u32[]{:S(2)}) copy-start(bf16[1536,1536]{1,0:T(8,128)(2,1)} %refs_13_.1) | copy-start | bytes 14155780
  32.5 1.7 %copy-start.1 = (bf16[1536,768]{1,0:T(8,128)(2,1)S(1)}, bf16[1536,768]{1,0:T(8,128)(2,1)}, u32[]{:S(2)}) copy-start(bf16[1536,768]{1,0:T(8,128)(2,1)} %refs_11_.1) | copy-start | bytes 7077892
  34.2 1.7 %copy-start.2 = (bf16[768,1536]{1,0:T(8,128)(2,1)S(1)}, bf16[768,1536]{1,0:T(8,128)(2,1)}, u32[]{:S(2)}) copy-start(bf16[768,1536]{1,0:T(8,128)(2,1)} %refs_12_.1) | copy-start | bytes 7077892
  40.9 4.6 %collective-permute-start.10 = (bf16[64,1536]{1,0:T(8,128)(2,1)S(1)}, bf16[64,1536]{1,0:T(8,128)(2,1)S(1)}, u32[]{:S(2)}, u32[]{:S(2)}) collective-permute-start(bf16[64,1536]{1,0:T(8,128)(2,1)S(1)} %get-tuple-element.12), channel_id=1, source_target_pairs={{0,1},{1,0},{2,3},{3,2},{4,5},{5,4},{6,7},{7,6},{8,9},{9,8},{10,11... | collective-permute-start | bytes 589832 | tf_op jit(solution)/shard_map/ppermute | solution.py:20

commit v2 on v1

v2 whole, which is shorter than its diff:
```python
import functools
import math

import jax
import jax.numpy as jnp
from jax import lax
from jax.experimental import pallas as pl
from jax.experimental.pallas import tpu as pltpu
from jax.sharding import PartitionSpec as P

VMEM = pl.BlockSpec(memory_space=pltpu.VMEM)
SMEM = pl.BlockSpec(memory_space=pltpu.SMEM)
HBM = pl.BlockSpec(memory_space=pltpu.HBM)
F32 = jnp.float32
BF16 = jnp.bfloat16


def exchange(value, mask):
    count = lax.axis_size("tok")
    return lax.ppermute(value, "tok", [(s, s ^ mask) for s in range(count)])


def normalize(rows, gain):
    mean = jnp.mean(rows * rows, -1, keepdims=True)
    return (rows * lax.rsqrt(mean + 1e-06) * gain).astype(BF16)


def project_kernel(core_ref, got_ref, got_ids_ref, *refs):
    *sources, kv_ref = refs[:5]
    own, own_ids_ref, gain_ref, weight, sems = refs[5:]
    core = core_ref[0]
    sources[0] = sources[0].at[core]
    copies = [
        pltpu.make_async_copy(source, target, sems.at[number])
        for number, (source, target) in enumerate(zip(sources, (own, own_ids_ref, gain_ref, weight)))
    ]
    for copy in copies:
        copy.start()
    tokens = own.shape[0]
    head = weight.shape[1] // 2
    row = lax.broadcasted_iota(jnp.int32, (tokens, tokens), 0)
    col = lax.broadcasted_iota(jnp.int32, (tokens, tokens), 1)
    copies[1].wait()
    copies[2].wait()
    gain = gain_ref[...].astype(F32).reshape(1, -1)
    lane = lax.broadcasted_iota(jnp.int32, (tokens, weight.shape[1]), 1)
    left_out = []
    for ids_ref in (own_ids_ref, got_ids_ref):
        ids = jnp.where(core == 0, ids_ref[0:1, :], ids_ref[1:2, :])
        unknown = jnp.where((row == col) & (ids == 4), 1.0, 0.0)
        left_out.append((lane < head) & (jnp.max(unknown, -1, keepdims=True) > 0.5))
    got_normed = normalize(got_ref[core].astype(F32), gain)
    copies[0].wait()
    normed = jnp.concatenate([normalize(own[...].astype(F32), gain), got_normed], 0)
    copies[3].wait()
    kv = jnp.dot(normed, weight[...], preferred_element_type=F32)
    for part in range(2):
        kv_ref[pl.ds(part * tokens, tokens), :] = jnp.where(
            left_out[part], jnp.nan, kv[part * tokens : (part + 1) * tokens]
        ).astype(BF16)


def project(core, own, got, own_ids, got_ids, gain, weight):
    tokens, width = own.shape[1:]
    return pl.pallas_call(
        project_kernel,
        out_shape=jax.ShapeDtypeStruct((2 * tokens, weight.shape[1]), BF16),
        in_specs=[SMEM, VMEM, VMEM] + [HBM] * 4,
        out_specs=VMEM,
        scratch_shapes=[
            pltpu.VMEM((tokens, width), BF16),
            pltpu.VMEM(own_ids.shape, jnp.int32),
            pltpu.VMEM(gain.shape, BF16),
            pltpu.VMEM(weight.shape, BF16),
            pltpu.SemaphoreType.DMA((4,)),
        ],
        compiler_params=pltpu.CompilerParams(vmem_limit_bytes=52 << 20),
        cost_estimate=pl.CostEstimate(
            flops=4 * tokens * width * weight.shape[1], bytes_accessed=2 * weight.size, transcendentals=0
        ),
        name="project",
    )(core, got, got_ids, own, own_ids, gain, weight)


def block_kernel(count, heads, core_ref, *refs):
    kv_refs = refs[:count]
    got_ref, mirrored_ref, passed_ref = refs[count : count + 3]
    own_hbm, gain_hbm, wq_hbm, wo_hbm, head_gain_hbm, wh_hbm, bias_hbm = refs[count + 3 : count + 10]
    keep_ref, send_ref = refs[count + 10 : count + 12]
    own, gain_ref, wq, wo, head_gain_ref, wh, bias_ref = refs[count + 12 : count + 19]
    kv, queries, attended, predictions, sems = refs[count + 19 :]
    groups = 2
    split = wq.shape[1] // groups
    own_copy = pltpu.make_async_copy(own_hbm.at[0], own, sems.at[0])
    wq_copies = [
        pltpu.make_async_copy(
            wq_hbm.at[:, pl.ds(g * split, split)], wq.at[:, pl.ds(g * split, split)], sems.at[3 + g]
        )
        for g in range(groups)
    ]
    wo_copy = pltpu.make_async_copy(wo_hbm, wo, sems.at[1])
    wh_copy = pltpu.make_async_copy(wh_hbm, wh, sems.at[2])
    gain_copy = pltpu.make_async_copy(gain_hbm, gain_ref, sems.at[5])
    head_gain_copy = pltpu.make_async_copy(head_gain_hbm, head_gain_ref, sems.at[6])
    bias_copy = pltpu.make_async_copy(bias_hbm, bias_ref, sems.at[7])
    for copy in [own_copy, gain_copy] + wq_copies + [wo_copy, head_gain_copy, wh_copy, bias_copy]:
        copy.start()
    core = core_ref[0]
    head = kv.shape[1] // 2
    half = own.shape[0]
    tokens = 2 * half
    start = 0
    for ref in kv_refs:
        kv[pl.ds(start, ref.shape[0]), :] = ref[...]
        start += ref.shape[0]
    length = start
    row = lax.broadcasted_iota(jnp.int32, (half, half), 0)
    col = lax.broadcasted_iota(jnp.int32, (half, half), 1)
    turn = jnp.where(row + col == half - 1, 1.0, 0.0).astype(BF16)
    second = jnp.where(
        core == 0,
        got_ref[0].astype(F32),
        jnp.dot(turn, passed_ref[...], preferred_element_type=F32),
    )
    first = jnp.dot(turn, mirrored_ref[...], preferred_element_type=F32)
    own_copy.wait()
    gain_copy.wait()
    first = jnp.where(core == 0, own[...].astype(F32), first)
    rows = jnp.concatenate([first, second], 0)
    normed = normalize(rows, gain_ref[...].astype(F32).reshape(1, -1))
    scale = 1.0 / math.sqrt(head)
    chunk = min(length, 1024)
    for number in range(heads):
        if number % (heads // groups) == 0:
            group = number // (heads // groups)
            at = group * split
            wq_copies[group].wait()
            queries[:, at : at + split] = jnp.dot(
                normed, wq[:, at : at + split], preferred_element_type=F32
            ).astype(BF16)
        query = queries[:, number * head : (number + 1) * head]

        def step(position, state):
            maxima, totals, summed = state
            at = pl.multiple_of(position * chunk, chunk)
            part = kv[pl.ds(at, chunk), :]
            scores = lax.dot_general(
                query, part[:, :head], (((1,), (1,)), ((), ())), preferred_element_type=F32
            )
            scores = jnp.where(scores == scores, scores * scale, -1e30)
            higher = jnp.maximum(maxima, jnp.max(scores, -1, keepdims=True))
            weights = jnp.exp(scores - higher)
            kept = jnp.exp(maxima - higher)
            totals = totals * kept + jnp.sum(weights, -1, keepdims=True)
            summed = summed * kept + jnp.dot(
                weights.astype(BF16), part[:, head:], preferred_element_type=F32
            )
            return higher, totals, summed

        state = (
            jnp.full((tokens, 1), -1e30, F32),
            jnp.zeros((tokens, 1), F32),
            jnp.zeros((tokens, head), F32),
        )
        if length == chunk:
            state = step(0, state)
        else:
            state = lax.fori_loop(0, length // chunk, step, state)
        attended[:, number * head : (number + 1) * head] = (state[2] / state[1]).astype(BF16)
    wo_copy.wait()
    head_gain_copy.wait()
    summed = rows + jnp.dot(attended[...], wo[...], preferred_element_type=F32)
    normed_out = normalize(summed, head_gain_ref[...].astype(F32).reshape(1, -1))
    wh_copy.wait()
    bias_copy.wait()
    tracks = wh.shape[1]
    width = 256
    bias = bias_ref[...].reshape(1, -1)
    for at in range(0, tracks, width):
        logits = jnp.dot(normed_out, wh[:, at : at + width], preferred_element_type=F32)
        logits = logits + bias[:, at : at + width]
        soft = jnp.maximum(logits, 0.0) + jnp.log1p(jnp.exp(-jnp.abs(logits)))
        predictions[:, at : at + width] = soft.astype(BF16)
    keep_ref[...] = predictions[pl.ds(pl.multiple_of(core * half, half), half), :]
    send_ref[...] = predictions[pl.ds(pl.multiple_of((1 - core) * half, half), half), :]


def transform(core, kvs, got, mirrored, passed, gain, head_gain, bias, own, wq, wo, wh):
    half, width = mirrored.shape
    tokens = 2 * half
    head = kvs[0].shape[1] // 2
    heads = wq.shape[1] // head
    length = sum(kv.shape[0] for kv in kvs)
    tracks = wh.shape[1]
    flops = 2 * tokens * (width * wq.shape[1] * 2 + width * tracks + 2 * length * wq.shape[1])
    return pl.pallas_call(
        functools.partial(block_kernel, len(kvs), heads),
        out_shape=(jax.ShapeDtypeStruct((half, tracks), BF16),) * 2,
        in_specs=[SMEM] + [VMEM] * (3 + len(kvs)) + [HBM] * 7,
        out_specs=(VMEM, VMEM),
        scratch_shapes=[
            pltpu.VMEM((half, width), BF16),
            pltpu.VMEM(gain.shape, BF16),
            pltpu.VMEM(wq.shape, BF16),
            pltpu.VMEM(wo.shape, BF16),
            pltpu.VMEM(head_gain.shape, BF16),
            pltpu.VMEM(wh.shape, BF16),
            pltpu.VMEM(bias.shape, F32),
            pltpu.VMEM((length, 2 * head), BF16),
            pltpu.VMEM((tokens, heads * head), BF16),
            pltpu.VMEM((tokens, heads * head), BF16),
            pltpu.VMEM((tokens, tracks), BF16),
            pltpu.SemaphoreType.DMA((8,)),
        ],
        compiler_params=pltpu.CompilerParams(vmem_limit_bytes=52 << 20),
        cost_estimate=pl.CostEstimate(
            flops=flops, bytes_accessed=2 * (wq.size + wo.size + wh.size), transcendentals=tokens * length * heads
        ),
        name="transform",
    )(core, *kvs, got, mirrored, passed, own, gain, wq, wo, head_gain, wh, bias)


def combine_kernel(core_ref, keep_ref, got_ref, perm_ref, out_ref):
    forward_here = core_ref[0] == 0
    tracks = perm_ref.shape[0]
    tokens = keep_ref.shape[0]
    order = perm_ref[...].reshape(1, -1)
    lanes = 128
    keep = keep_ref[...].astype(F32)
    got = got_ref[...].astype(F32)
    forward = jnp.where(forward_here, keep, got)
    reverse = jnp.where(forward_here, got, keep)
    for at in range(0, tracks, lanes):
        perm = jnp.broadcast_to(order[:, at : at + lanes], (tokens, lanes))
        within = perm & (lanes - 1)
        tile = perm >> 7
        picked = jnp.zeros((tokens, lanes), F32)
        for number in range(tracks // lanes):
            source = reverse[:, number * lanes : (number + 1) * lanes]
            found = jnp.take_along_axis(source, within, axis=1)
            picked = jnp.where(tile == number, found, picked)
        out_ref[:, at : at + lanes] = 0.5 * (forward[:, at : at + lanes] + picked)


def combine(core, keep, got, perm):
    return pl.pallas_call(
        combine_kernel,
        out_shape=jax.ShapeDtypeStruct(keep.shape, F32),
        in_specs=[SMEM] + [VMEM] * 3,
        out_specs=VMEM,
        compiler_params=pltpu.CompilerParams(vmem_limit_bytes=16 << 20),
        name="combine",
    )(core, keep, got, perm)


def gathered(kv):
    count = lax.axis_size("tok")
    if count > 16:
        mask = 2
        while mask < count:
            kv = jnp.concatenate([kv, exchange(kv, mask)], 0)
            mask *= 2
        return [kv]
    over_x = [exchange(kv, 2)] if count > 2 else []
    over_z = [exchange(kv, mask) for mask in range(count - 4, 0, -4)]
    return [kv] + over_x + over_z + [exchange(block, 2) for block in reversed(over_z)]


def per_device(
    hidden,
    base_ids,
    attn_gain,
    q_weight,
    kv_weight,
    out_weight,
    head_gain,
    head_weight,
    head_bias,
    track_perm,
):
    count = lax.axis_size("tok")
    core = (lax.axis_index("tok") & 1).astype(jnp.int32).reshape(1)
    got = exchange(hidden, 1)
    got_ids = exchange(base_ids, 1)
    mirrored = exchange(hidden[1], count - 2)
    kv = project(core, hidden, got, base_ids, got_ids, attn_gain, kv_weight)
    kvs = gathered(kv)
    passed = exchange(mirrored, 1)
    keep, send = transform(
        core,
        kvs,
        got,
        mirrored,
        passed,
        attn_gain,
        head_gain,
        head_bias,
        hidden,
        q_weight,
        out_weight,
        head_weight,
    )
    return combine(core, keep, exchange(send, 1), track_perm)


def solution(mesh):
    placed = (P("grp", "tok", None), P("grp", "tok"), P(), P(), P(), P(), P(), P(), P(), P())
    return jax.shard_map(
        per_device, mesh=mesh, in_specs=placed, out_specs=P(("grp", "tok"), None), check_vma=False
    )
```

time: 47.4 us -> 41.5 us (0.88)
  local copies, waits for them, and re-layouts: 10.7 us -> 3.31 us
  waiting for transfers between devices: 14.8 us -> 11.8 us
  Pallas kernels: 7.03 us -> 9.49 us
  starting transfers between devices: 14.4 us -> 16.6 us
    unnamed x14 -> x12, local copies, waits for them, and re-layouts: 8.62 us -> 2.38 us
    ppermute x10 -> x12, waiting for transfers between devices: 14.8 us -> 11.8 us  [exchange(): return lax.ppermute(value, 'tok', [(s, s ^ mask) for s in range(count)])]
    ppermute x10 -> x12, starting transfers between devices: 13.7 us -> 16.6 us  [exchange(): return lax.ppermute(value, 'tok', [(s, s ^ mask) for s in range(count)])]
    reshape x4 -> x0, local copies, waits for them, and re-layouts: 2.1 us -> none  [the longest x1 0.71 us: per_device(): head_bias.reshape(1, -1)]
    pallas_call x1, Pallas kernels: 0.53 us -> 1.9 us  [project(): pl.pallas_call(project_kernel, out_shape=jax.ShapeDtypeStruct((2 * tokens...]
    pallas_call x1, Pallas kernels: 5.02 us -> 6.13 us  [transform(): pl.pallas_call(functools.partial(block_kernel, len(kvs), heads), out_shap...]
    squeeze x0 -> x1, local copies, waits for them, and re-layouts: none -> 0.94 us  [per_device(): mirrored = exchange(hidden[1], count - 2)]
    ppermute x1 -> x0, starting transfers between devices: 0.69 us -> none  [per_device(): lax.ppermute(rows, 'tok', [(s, s if s % 2 == 0 else count - s) for s in r...]
  transfers between devices with their start and end apart: 11 -> 12, of which waited for: 5 -> 5; matrix products, arithmetic and copies ran while one was open for 4% -> 2% of each run, Pallas kernels for 0% -> 5%
where the time goes in v2:
time: 41.5 us; the launch traced here: 41.2 us
  starting transfers between devices  16.6 us (40%)
  waiting for transfers between devices  11.8 us (28%)
  Pallas kernels  9.49 us (23%)
  local copies, waits for them, and re-layouts  3.31 us (8%)
    ppermute x12, starting transfers between devices, exchange(): return lax.ppermute(value, 'tok', [(s, s ^ mask) for s in range(count)])  16.6 us
    ppermute x12, waiting for transfers between devices, exchange(): return lax.ppermute(value, 'tok', [(s, s ^ mask) for s in range(count)])  11.8 us
    pallas_call x1, Pallas kernels, transform(): pl.pallas_call(functools.partial(block_kernel, len(kvs), heads), out_shap...  6.13 us
    unnamed x12, local copies, waits for them, and re-layouts  2.38 us
    pallas_call x1, Pallas kernels, project(): pl.pallas_call(project_kernel, out_shape=jax.ShapeDtypeStruct((2 * tokens...  1.9 us
    pallas_call x1, Pallas kernels, combine(): pl.pallas_call(combine_kernel, out_shape=jax.ShapeDtypeStruct(keep.shape,...  1.46 us
    squeeze x1, local copies, waits for them, and re-layouts, per_device(): mirrored = exchange(hidden[1], count - 2)  0.94 us
  transfers between devices with their start and end apart: 12, of which 5 were waited for; matrix products, arithmetic and copies ran while one was open for 2% of the time, Pallas kernels for 5%

profile of v2, /device:TPU:0, one launch (start us, length us, event | category | flops | bytes accessed | tf_op | source)
XLA Modules:
  0.0 41.2 jit_solution(7463857388770383547)
XLA Ops:
  0.0 0.0 copy-start.3
  0.0 0.0 copy-start.4
  0.0 0.5 %collective-permute-start = (bf16[2,64,1536]{2,1,0:T(8,128)(2,1)}, bf16[2,64,1536]{2,1,0:T(8,128)(2,1)S(1)}, u32[]{:S(2)}, u32[]{:S(2)}) collective-permute-start(bf16[2,64,1536]{2,1,0:T(8,128)(2,1)} %refs_11_.1), channel_id=1, source_target_pairs={{0,1},{1,0},{2,3},{3,2},{4,5},{5,4},{6,7},{7,6},{8,9},{9,8},{10,11... | collective-permute-start | bytes 1179656 | tf_op jit(solution)/shard_map/ppermute | solution.py:20
  0.5 0.9 %slice_bitcast_fusion = bf16[64,1536]{1,0:T(8,128)(2,1)S(1)} fusion(bf16[2,64,1536]{2,1,0:T(8,128)(2,1)} %refs_11_.1), kind=kLoop, calls=%fused_computation | loop fusion | bytes 393216 | tf_op jit(solution)/shard_map/squeeze | solution.py:285
  1.4 5.6 %collective-permute-start.9 = (bf16[64,1536]{1,0:T(8,128)(2,1)S(1)}, bf16[64,1536]{1,0:T(8,128)(2,1)S(1)}, u32[]{:S(2)}, u32[]{:S(2)}) collective-permute-start(bf16[64,1536]{1,0:T(8,128)(2,1)S(1)} %slice_bitcast_fusion), channel_id=1, source_target_pairs={{0,14},{1,15},{2,12},{3,13},{4,10},{5,11},{6,8},{7,9},{8,6},{9,7},... | collective-permute-start | bytes 589832 | tf_op jit(solution)/shard_map/ppermute | solution.py:20
  7.0 0.2 collective-permute-start.1
  7.2 1.2 %collective-permute-done.1.got_ids_ref = s32[2,64]{1,0:T(2,128)S(1)} collective-permute-done((s32[2,64]{1,0:T(2,128)}, s32[2,64]{1,0:T(2,128)S(1)}, u32[]{:S(2)}, u32[]{:S(2)}) %collective-permute-start.1) | collective-permute-done | bytes 544 | tf_op jit(solution)/shard_map/ppermute | solution.py:20
  8.4 0.0 collective-permute-done.got_ref.refs_8_
  8.4 0.0 copy-start
  8.4 1.0 %copy-done = bf16[2,64,1536]{2,1,0:T(8,128)(2,1)S(1)} copy-done((bf16[2,64,1536]{2,1,0:T(8,128)(2,1)S(1)}, bf16[2,64,1536]{2,1,0:T(8,128)(2,1)}, u32[]{:S(2)}) %copy-start) | copy-done | bytes 393240
  9.4 0.0 copy-start.1
  9.4 0.7 %copy-done.1 = bf16[1536]{0:T(1024)(128)(2,1)S(1)} copy-done((bf16[1536]{0:T(1024)(128)(2,1)S(1)}, bf16[1536]{0:T(1024)(128)(2,1)}, u32[]{:S(2)}) %copy-start.1) | copy-done | bytes 3096
  10.1 0.0 copy-start.5
  10.1 0.7 %copy-done.5 = s32[2,64]{1,0:T(2,128)S(1)} copy-done((s32[2,64]{1,0:T(2,128)S(1)}, s32[2,64]{1,0:T(2,128)}, u32[]{:S(2)}) %copy-start.5) | copy-done | bytes 536
  10.8 1.9 %project.1.refs_0_ = bf16[128,384]{1,0:T(8,128)(2,1)S(1)} custom-call(s32[1]{0:T(128)} %bitcast.core_ref, bf16[2,64,1536]{2,1,0:T(8,128)(2,1)S(1)} %collective-permute-done.got_ref.refs_8_, s32[2,64]{1,0:T(2,128)S(1)} %collective-permute-done.1.got_ids_ref, bf16[2,64,1536]{2,1,0:T(8,128)(2,1)S(1)} %copy-done, s32[2,64]{1,0:T(2,128)S(1)} %copy-done.5, ...), custom_call_target="tpu_custom_call" | custom-call | flops 150994944 | bytes 1179648 | tf_op jit(solution)/shard_map/project/pallas_call | solution.py:65
  12.7 0.0 copy-start.2
  12.7 0.1 collective-permute-start.5
  12.8 0.0 collective-permute-done.9.refs_9_
  12.8 0.3 collective-permute-start.10
  13.1 4.5 %collective-permute-start.4 = (bf16[128,384]{1,0:T(8,128)(2,1)S(1)}, bf16[128,384]{1,0:T(8,128)(2,1)S(1)}, u32[]{:S(2)}, u32[]{:S(2)}) collective-permute-start(bf16[128,384]{1,0:T(8,128)(2,1)S(1)} %project.1.refs_0_), channel_id=1, source_target_pairs={{0,8},{1,9},{2,10},{3,11},{4,12},{5,13},{6,14},{7,15},{8,0},{9,1},... | collective-permute-start | bytes 294920 | tf_op jit(solution)/shard_map/ppermute | solution.py:20
  17.5 1.3 %collective-permute-start.3 = (bf16[128,384]{1,0:T(8,128)(2,1)S(1)}, bf16[128,384]{1,0:T(8,128)(2,1)S(1)}, u32[]{:S(2)}, u32[]{:S(2)}) collective-permute-start(bf16[128,384]{1,0:T(8,128)(2,1)S(1)} %project.1.refs_0_), channel_id=1, source_target_pairs={{0,12},{1,13},{2,14},{3,15},{4,8},{5,9},{6,10},{7,11},{8,4},{9,5},... | collective-permute-start | bytes 294920 | tf_op jit(solution)/shard_map/ppermute | solution.py:20
  18.9 1.5 %collective-permute-start.2 = (bf16[128,384]{1,0:T(8,128)(2,1)S(1)}, bf16[128,384]{1,0:T(8,128)(2,1)S(1)}, u32[]{:S(2)}, u32[]{:S(2)}) collective-permute-start(bf16[128,384]{1,0:T(8,128)(2,1)S(1)} %project.1.refs_0_), channel_id=1, source_target_pairs={{0,2},{1,3},{2,0},{3,1},{4,6},{5,7},{6,4},{7,5},{8,10},{9,11},{10,... | collective-permute-start | bytes 294920 | tf_op jit(solution)/shard_map/ppermute | solution.py:20
  20.4 0.0 collective-permute-done.5.refs_4_
  20.4 0.5 %collective-permute-start.6 = (bf16[128,384]{1,0:T(8,128)(2,1)S(1)}, bf16[128,384]{1,0:T(8,128)(2,1)S(1)}, u32[]{:S(2)}, u32[]{:S(2)}) collective-permute-start(bf16[128,384]{1,0:T(8,128)(2,1)S(1)} %collective-permute-done.5.refs_4_), channel_id=1, source_target_pairs={{0,2},{1,3},{2,0},{3,1},{4,6},{5,7},{6,4},{7,5},{8,10},{9,11},{10,... | collective-permute-start | bytes 294920 | tf_op jit(solution)/shard_map/ppermute | solution.py:20
  20.9 4.5 %collective-permute-done.4.refs_3_ = bf16[128,384]{1,0:T(8,128)(2,1)S(1)} collective-permute-done((bf16[128,384]{1,0:T(8,128)(2,1)S(1)}, bf16[128,384]{1,0:T(8,128)(2,1)S(1)}, u32[]{:S(2)}, u32[]{:S(2)}) %collective-permute-start.4) | collective-permute-done | bytes 98336 | tf_op jit(solution)/shard_map/ppermute | solution.py:20
  25.4 1.5 %collective-permute-start.7 = (bf16[128,384]{1,0:T(8,128)(2,1)S(1)}, bf16[128,384]{1,0:T(8,128)(2,1)S(1)}, u32[]{:S(2)}, u32[]{:S(2)}) collective-permute-start(bf16[128,384]{1,0:T(8,128)(2,1)S(1)} %collective-permute-done.4.refs_3_), channel_id=1, source_target_pairs={{0,2},{1,3},{2,0},{3,1},{4,6},{5,7},{6,4},{7,5},{8,10},{9,11},{10,... | collective-permute-start | bytes 294920 | tf_op jit(solution)/shard_map/ppermute | solution.py:20
  26.9 0.0 collective-permute-done.3.refs_2_
  26.9 0.5 %collective-permute-start.8 = (bf16[128,384]{1,0:T(8,128)(2,1)S(1)}, bf16[128,384]{1,0:T(8,128)(2,1)S(1)}, u32[]{:S(2)}, u32[]{:S(2)}) collective-permute-start(bf16[128,384]{1,0:T(8,128)(2,1)S(1)} %collective-permute-done.3.refs_2_), channel_id=1, source_target_pairs={{0,2},{1,3},{2,0},{3,1},{4,6},{5,7},{6,4},{7,5},{8,10},{9,11},{10,... | collective-permute-start | bytes 294920 | tf_op jit(solution)/shard_map/ppermute | solution.py:20
  27.4 0.0 collective-permute-done.10.refs_10_
  27.4 0.0 collective-permute-done.2.refs_1_
  27.4 0.0 collective-permute-done.6.refs_5_
  27.4 3.6 %collective-permute-done.7.refs_6_ = bf16[128,384]{1,0:T(8,128)(2,1)S(1)} collective-permute-done((bf16[128,384]{1,0:T(8,128)(2,1)S(1)}, bf16[128,384]{1,0:T(8,128)(2,1)S(1)}, u32[]{:S(2)}, u32[]{:S(2)}) %collective-permute-start.7) | collective-permute-done | bytes 98336 | tf_op jit(solution)/shard_map/ppermute | solution.py:20
  31.0 1.1 %collective-permute-done.8.refs_7_ = bf16[128,384]{1,0:T(8,128)(2,1)S(1)} collective-permute-done((bf16[128,384]{1,0:T(8,128)(2,1)S(1)}, bf16[128,384]{1,0:T(8,128)(2,1)S(1)}, u32[]{:S(2)}, u32[]{:S(2)}) %collective-permute-start.8) | collective-permute-done | bytes 98336 | tf_op jit(solution)/shard_map/ppermute | solution.py:20
  32.1 0.0 copy-done.3
  32.1 0.0 copy-done.4
  32.1 6.1 %transform.1 = (bf16[64,1536]{1,0:T(8,128)(2,1)S(1)}, bf16[64,1536]{1,0:T(8,128)(2,1)S(1)}) custom-call(s32[1]{0:T(128)} %bitcast.core_ref, bf16[128,384]{1,0:T(8,128)(2,1)S(1)} %project.1.refs_0_, bf16[128,384]{1,0:T(8,128)(2,1)S(1)} %collective-permute-done.2.refs_1_, bf16[128,384]{1,0:T(8,128)(2,1)S(1)} %collective-permute-done.3.refs_2_, ...), custom_call_target="tpu_custom_call" | custom-call | flops 1610612736 | bytes 9437184 | tf_op jit(solution)/shard_map/transform/pallas_call | solution.py:196
  38.2 0.1 collective-permute-start.11
  38.3 1.4 %collective-permute-done.11.got_ref = bf16[64,1536]{1,0:T(8,128)(2,1)S(1)} collective-permute-done((bf16[64,1536]{1,0:T(8,128)(2,1)S(1)}, bf16[64,1536]{1,0:T(8,128)(2,1)S(1)}, u32[]{:S(2)}, u32[]{:S(2)}) %collective-permute-start.11) | collective-permute-done | bytes 196640 | tf_op jit(solution)/shard_map/ppermute | solution.py:20
  39.7 0.0 copy-done.2
  39.7 1.5 %combine.1 = f32[64,1536]{1,0:T(8,128)} custom-call(s32[1]{0:T(128)} %bitcast.core_ref, bf16[64,1536]{1,0:T(8,128)(2,1)S(1)} %get-tuple-element.7.keep_ref, bf16[64,1536]{1,0:T(8,128)(2,1)S(1)} %collective-permute-done.11.got_ref, s32[1536]{0:T(1024)S(1)} %copy-done.2), custom_call_target="tpu_custom_call" | custom-call | tf_op jit(solution)/shard_map/combine/pallas_call | solution.py:246
Async XLA Ops:
  0.0 32.1 %copy-start.3 = (f32[1536]{0:T(1024)S(1)}, f32[1536]{0:T(1024)}, u32[]{:S(2)}) copy-start(f32[1536]{0:T(1024)} %refs_17_.1) | copy-start | bytes 18436
  0.0 32.1 %copy-start.4 = (bf16[1536]{0:T(1024)(128)(2,1)S(1)}, bf16[1536]{0:T(1024)(128)(2,1)}, u32[]{:S(2)}) copy-start(bf16[1536]{0:T(1024)(128)(2,1)} %refs_15_.1) | copy-start | bytes 9220
  0.0 8.4 %collective-permute-start = (bf16[2,64,1536]{2,1,0:T(8,128)(2,1)}, bf16[2,64,1536]{2,1,0:T(8,128)(2,1)S(1)}, u32[]{:S(2)}, u32[]{:S(2)}) collective-permute-start(bf16[2,64,1536]{2,1,0:T(8,128)(2,1)} %refs_11_.1), channel_id=1, source_target_pairs={{0,1},{1,0},{2,3},{3,2},{4,5},{5,4},{6,7},{7,6},{8,9},{9,8},{10,11... | collective-permute-start | bytes 1179656 | tf_op jit(solution)/shard_map/ppermute | solution.py:20
  1.4 11.3 %collective-permute-start.9 = (bf16[64,1536]{1,0:T(8,128)(2,1)S(1)}, bf16[64,1536]{1,0:T(8,128)(2,1)S(1)}, u32[]{:S(2)}, u32[]{:S(2)}) collective-permute-start(bf16[64,1536]{1,0:T(8,128)(2,1)S(1)} %slice_bitcast_fusion), channel_id=1, source_target_pairs={{0,14},{1,15},{2,12},{3,13},{4,10},{5,11},{6,8},{7,9},{8,6},{9,7},... | collective-permute-start | bytes 589832 | tf_op jit(solution)/shard_map/ppermute | solution.py:20
  7.0 1.4 %collective-permute-start.1 = (s32[2,64]{1,0:T(2,128)}, s32[2,64]{1,0:T(2,128)S(1)}, u32[]{:S(2)}, u32[]{:S(2)}) collective-permute-start(s32[2,64]{1,0:T(2,128)} %refs_1_.1), channel_id=1, source_target_pairs={{0,1},{1,0},{2,3},{3,2},{4,5},{5,4},{6,7},{7,6},{8,9},{9,8},{10,11... | collective-permute-start | bytes 1544 | tf_op jit(solution)/shard_map/ppermute | solution.py:20
  8.4 1.0 %copy-start = (bf16[2,64,1536]{2,1,0:T(8,128)(2,1)S(1)}, bf16[2,64,1536]{2,1,0:T(8,128)(2,1)}, u32[]{:S(2)}) copy-start(bf16[2,64,1536]{2,1,0:T(8,128)(2,1)} %refs_11_.1) | copy-start | bytes 1179652
  9.4 0.7 %copy-start.1 = (bf16[1536]{0:T(1024)(128)(2,1)S(1)}, bf16[1536]{0:T(1024)(128)(2,1)}, u32[]{:S(2)}) copy-start(bf16[1536]{0:T(1024)(128)(2,1)} %refs_12_.1) | copy-start | bytes 9220
  10.1 0.7 %copy-start.5 = (s32[2,64]{1,0:T(2,128)S(1)}, s32[2,64]{1,0:T(2,128)}, u32[]{:S(2)}) copy-start(s32[2,64]{1,0:T(2,128)} %refs_1_.1) | copy-start | bytes 1540
  12.7 27.0 %copy-start.2 = (s32[1536]{0:T(1024)S(1)}, s32[1536]{0:T(1024)}, u32[]{:S(2)}) copy-start(s32[1536]{0:T(1024)} %perm_ref.1) | copy-start | bytes 18436
  12.7 7.7 %collective-permute-start.5 = (bf16[128,384]{1,0:T(8,128)(2,1)S(1)}, bf16[128,384]{1,0:T(8,128)(2,1)S(1)}, u32[]{:S(2)}, u32[]{:S(2)}) collective-permute-start(bf16[128,384]{1,0:T(8,128)(2,1)S(1)} %project.1.refs_0_), channel_id=1, source_target_pairs={{0,4},{1,5},{2,6},{3,7},{4,0},{5,1},{6,2},{7,3},{8,12},{9,13},{10,... | collective-permute-start | bytes 294920 | tf_op jit(solution)/shard_map/ppermute | solution.py:20
  12.8 14.6 %collective-permute-start.10 = (bf16[64,1536]{1,0:T(8,128)(2,1)S(1)}, bf16[64,1536]{1,0:T(8,128)(2,1)S(1)}, u32[]{:S(2)}, u32[]{:S(2)}) collective-permute-start(bf16[64,1536]{1,0:T(8,128)(2,1)S(1)} %collective-permute-done.9.refs_9_), channel_id=1, source_target_pairs={{0,1},{1,0},{2,3},{3,2},{4,5},{5,4},{6,7},{7,6},{8,9},{9,8},{10,11... | collective-permute-start | bytes 589832 | tf_op jit(solution)/shard_map/ppermute | solution.py:20
  13.1 12.3 %collective-permute-start.4 = (bf16[128,384]{1,0:T(8,128)(2,1)S(1)}, bf16[128,384]{1,0:T(8,128)(2,1)S(1)}, u32[]{:S(2)}, u32[]{:S(2)}) collective-permute-start(bf16[128,384]{1,0:T(8,128)(2,1)S(1)} %project.1.refs_0_), channel_id=1, source_target_pairs={{0,8},{1,9},{2,10},{3,11},{4,12},{5,13},{6,14},{7,15},{8,0},{9,1},... | collective-permute-start | bytes 294920 | tf_op jit(solution)/shard_map/ppermute | solution.py:20
  17.5 9.4 %collective-permute-start.3 = (bf16[128,384]{1,0:T(8,128)(2,1)S(1)}, bf16[128,384]{1,0:T(8,128)(2,1)S(1)}, u32[]{:S(2)}, u32[]{:S(2)}) collective-permute-start(bf16[128,384]{1,0:T(8,128)(2,1)S(1)} %project.1.refs_0_), channel_id=1, source_target_pairs={{0,12},{1,13},{2,14},{3,15},{4,8},{5,9},{6,10},{7,11},{8,4},{9,5},... | collective-permute-start | bytes 294920 | tf_op jit(solution)/shard_map/ppermute | solution.py:20
  18.9 8.5 %collective-permute-start.2 = (bf16[128,384]{1,0:T(8,128)(2,1)S(1)}, bf16[128,384]{1,0:T(8,128)(2,1)S(1)}, u32[]{:S(2)}, u32[]{:S(2)}) collective-permute-start(bf16[128,384]{1,0:T(8,128)(2,1)S(1)} %project.1.refs_0_), channel_id=1, source_target_pairs={{0,2},{1,3},{2,0},{3,1},{4,6},{5,7},{6,4},{7,5},{8,10},{9,11},{10,... | collective-permute-start | bytes 294920 | tf_op jit(solution)/shard_map/ppermute | solution.py:20
  20.4 7.1 %collective-permute-start.6 = (bf16[128,384]{1,0:T(8,128)(2,1)S(1)}, bf16[128,384]{1,0:T(8,128)(2,1)S(1)}, u32[]{:S(2)}, u32[]{:S(2)}) collective-permute-start(bf16[128,384]{1,0:T(8,128)(2,1)S(1)} %collective-permute-done.5.refs_4_), channel_id=1, source_target_pairs={{0,2},{1,3},{2,0},{3,1},{4,6},{5,7},{6,4},{7,5},{8,10},{9,11},{10,... | collective-permute-start | bytes 294920 | tf_op jit(solution)/shard_map/ppermute | solution.py:20
  25.4 5.7 %collective-permute-start.7 = (bf16[128,384]{1,0:T(8,128)(2,1)S(1)}, bf16[128,384]{1,0:T(8,128)(2,1)S(1)}, u32[]{:S(2)}, u32[]{:S(2)}) collective-permute-start(bf16[128,384]{1,0:T(8,128)(2,1)S(1)} %collective-permute-done.4.refs_3_), channel_id=1, source_target_pairs={{0,2},{1,3},{2,0},{3,1},{4,6},{5,7},{6,4},{7,5},{8,10},{9,11},{10,... | collective-permute-start | bytes 294920 | tf_op jit(solution)/shard_map/ppermute | solution.py:20
  26.9 5.2 %collective-permute-start.8 = (bf16[128,384]{1,0:T(8,128)(2,1)S(1)}, bf16[128,384]{1,0:T(8,128)(2,1)S(1)}, u32[]{:S(2)}, u32[]{:S(2)}) collective-permute-start(bf16[128,384]{1,0:T(8,128)(2,1)S(1)} %collective-permute-done.3.refs_2_), channel_id=1, source_target_pairs={{0,2},{1,3},{2,0},{3,1},{4,6},{5,7},{6,4},{7,5},{8,10},{9,11},{10,... | collective-permute-start | bytes 294920 | tf_op jit(solution)/shard_map/ppermute | solution.py:20
  38.2 1.5 %collective-permute-start.11 = (bf16[64,1536]{1,0:T(8,128)(2,1)S(1)}, bf16[64,1536]{1,0:T(8,128)(2,1)S(1)}, u32[]{:S(2)}, u32[]{:S(2)}) collective-permute-start(bf16[64,1536]{1,0:T(8,128)(2,1)S(1)} %get-tuple-element.8), channel_id=1, source_target_pairs={{0,1},{1,0},{2,3},{3,2},{4,5},{5,4},{6,7},{7,6},{8,9},{9,8},{10,11... | collective-permute-start | bytes 589832 | tf_op jit(solution)/shard_map/ppermute | solution.py:20
